TPU v7x, 512 devices: a whole 4x8x8 slice. The times are simulated.
512 devices in a mesh: grp: 16 (over z_lo, y), dev: 32 (over x, z_hi, core).
Axes of the slice: x: 4, y: 8, z: 8 (z_hi: 4, z_lo: 2; z = z_hi * 2 + z_lo), core: 2. Of those that a mesh axis runs over, the one named last changes fastest.
Arguments:
- sketch: bfloat16 [1048576, 256], P(('grp', 'dev')), may hold values from -4 to 4
- marginal_std: float32 [1048576], P(('grp', 'dev')), may hold values from 0.1 to 10
- cov_tiles: bfloat16 [9, 256, 256], replicated, may hold values from 0 to 1
- tile_cols: int32 [4096, 9], P(('grp', 'dev')), may hold values from -1 to 4095, as said below
Outputs:
- basis: float32 [1048576, 256], P(('grp', 'dev'))
- factor: float32 [256, 256], replicated
Inputs may be any that keep to these rules, and one draw needn't show every extreme that they name: `tile_cols`: tile t holds one line of 256 cells. The lines lie in depth order, except that the order within each aligned block of 4 tiles is permuted. Entry e of the list of tile t is the tile that holds the line e - 4 lines from the line of t (entry 4 is t itself), or -1 where that line lies beyond the ends of the field.
All inputs are finite; a program needn't handle non-finite values.
Results may differ from a plain program's by a relative error of at most 0.0035.
Values may be sent and summed in bfloat16 or wider, within the bound.
A program may use at most 64 MiB of HBM per device.

v0:
```python
import jax
import jax.numpy as jnp
from jax import lax
from jax.sharding import PartitionSpec as P


def with_halo(block, sides, width):
    for axis, dim in sides:
        count = lax.axis_size(axis)
        forward = [(i, i + 1) for i in range(count - 1)]
        backward = [(target, source) for source, target in forward]
        low = lax.ppermute(
            lax.slice_in_dim(block, block.shape[dim] - width, None, axis=dim), axis, forward
        )
        high = lax.ppermute(lax.slice_in_dim(block, 0, width, axis=dim), axis, backward)
        block = jnp.concatenate([low, block, high], axis=dim)
    return block


def per_device(sketch, marginal_std, cov_tiles, tile_cols):
    row_count, column_count = sketch.shape
    tile_size = cov_tiles.shape[1]
    row_tiles = row_count // tile_size
    scaled = (sketch.astype(jnp.float32) * marginal_std[:, None]).astype(jnp.bfloat16)
    extended = with_halo(scaled, ((("grp", "dev"), 0),), row_tiles * tile_size)
    extended_tiles = extended.reshape(-1, tile_size, column_count)
    first_tile = lax.axis_index(("grp", "dev")) * row_tiles
    present = tile_cols >= 0
    local_cols = jnp.where(present, tile_cols - first_tile + row_tiles, 0)
    gathered = extended_tiles[local_cols.T]
    gathered = jnp.where(present.T[:, :, None, None], gathered, jnp.zeros((), jnp.bfloat16))
    products = jnp.einsum("eij,etjk->tik", cov_tiles, gathered, preferred_element_type=jnp.float32)
    latent_field = products.reshape(row_count, column_count) * marginal_std[:, None]
    total_rows = row_count * lax.axis_size("grp") * lax.axis_size("dev")
    gram_matrix = (
        jnp.dot(latent_field.T, latent_field, precision=lax.Precision.HIGHEST) / total_rows
    )
    gram_matrix = lax.psum(gram_matrix, ("grp", "dev"))
    lower_factor = jnp.linalg.cholesky(gram_matrix)
    basis = lax.linalg.triangular_solve(
        lower_factor, latent_field, left_side=False, lower=True, transpose_a=True
    )
    return (basis, lower_factor.T)


def solution(mesh):
    in_specs = (P(("grp", "dev"), None), P(("grp", "dev")), P(), P(("grp", "dev"), None))
    out_specs = (P(("grp", "dev"), None), P())
    return jax.shard_map(
        per_device, mesh=mesh, in_specs=in_specs, out_specs=out_specs, check_vma=False
    )
```

profile of v0, /device:TPU:23, one launch (start us, length us, event | category | flops | bytes accessed | tf_op | source)
XLA Modules:
  0.0 430.0 jit_solution(10741237708848555990)
XLA Ops:
  7.2 0.0 copy-start
  7.2 0.0 copy-start.7
  7.2 0.0 copy-start.8
  7.2 0.0 all-reduce.3.cloned.1.call-start
  7.2 1.6 multiply_convert_fusion
  8.9 6.4 %collective-permute-start = (bf16[2048,256]{1,0:T(8,128)(2,1)S(1)}, bf16[2048,256]{1,0:T(8,128)(2,1)S(1)}, u32[]{:S(2)}, u32[]{:S(2)}) collective-permute-start(bf16[2048,256]{1,0:T(8,128)(2,1)S(1)} %multiply_convert_fusion), channel_id=1, source_target_pairs={{0,1},{1,2},{2,3},{3,4},{4,5},{5,6},{6,7},{7,8},{8,9},{9,10},{10,1... | collective-permute-start | bytes 3145736 | tf_op jit(solution)/shard_map/ppermute | solution.py:12
  15.3 1.9 collective-permute-start.1
  17.2 0.0 copy-done.7
  17.2 0.0 copy-done.8
  17.3 0.1 copy.13
  17.4 0.1 reshape.62
  17.4 0.1 copy.12
  17.6 15.5 %collective-permute-done = bf16[2048,256]{1,0:T(8,128)(2,1)S(1)} collective-permute-done((bf16[2048,256]{1,0:T(8,128)(2,1)S(1)}, bf16[2048,256]{1,0:T(8,128)(2,1)S(1)}, u32[]{:S(2)}, u32[]{:S(2)}) %collective-permute-start) | collective-permute-done | bytes 1048608 | tf_op jit(solution)/shard_map/ppermute | solution.py:12
  33.0 10.8 %collective-permute-done.1 = bf16[2048,256]{1,0:T(8,128)(2,1)} collective-permute-done((bf16[2048,256]{1,0:T(8,128)(2,1)S(1)}, bf16[2048,256]{1,0:T(8,128)(2,1)}, u32[]{:S(2)}, u32[]{:S(2)}) %collective-permute-start.1) | collective-permute-done | bytes 1048608 | tf_op jit(solution)/shard_map/ppermute | solution.py:15
  43.8 2.8 pad_maximum_fusion
  46.7 7.8 %gather_fusion = bf16[72,256,256]{2,1,0:T(8,128)(2,1)} fusion(bf16[24,256,256]{2,1,0:T(8,128)(2,1)} %bitcast.60, s32[1024]{0:T(1024)S(1)} %pad_clamp_fusion), kind=kCustom, calls=%fused_computation | custom fusion | bytes 18874656 | tf_op jit(solution)/shard_map/gather | solution.py:30
  54.5 0.0 copy-done
  54.5 5.5 %fusion = f32[8,256,256,1]{1,2,0,3:T(8,128)S(1)} fusion(bf16[9,8,256,256]{3,2,1,0:T(8,128)(2,1)} %bitcast.61, pred[9,8]{1,0:T(8,128)(4,1)S(1)} %copy.12, bf16[9,256,256]{2,1,0:T(8,128)(2,1)S(1)} %copy-done), kind=kOutput, calls=%fused_computation.3 | convolution fusion | flops 2420637696 | bytes 12714056 | tf_op jit(solution)/shard_map/eij,etjk->tik/dot_general | solution.py:32
  59.9 0.0 copy-start.1
  60.0 1.3 copy-done.1
  61.3 4.8 %fusion.7 = f32[256,256]{0,1:T(8,128)} fusion(f32[8,256,256,1]{1,2,0,3:T(8,128)S(1)} %fusion, f32[8,256]{1,0:T(8,128)S(1)} %mul.33), kind=kOutput, calls=%fused_computation.16 | convolution fusion | flops 1611202560 | bytes 2367488 | tf_op jit(solution)/shard_map/dot_general | solution.py:36
  66.1 0.0 all-reduce.3.cloned.1.call-update
  66.1 1.9 bitcast_multiply_fusion
  68.0 273.6 %all-reduce.3.cloned.1.call-done = f32[256,256]{0,1:T(8,128)} async-done(((f32[256,256]{0,1:T(8,128)}), f32[256,256]{0,1:T(8,128)}) %all-reduce.3.cloned.1.call-update) | async-done | bytes 262160 | tf_op jit(solution)/shard_map/psum | solution.py:38
  341.6 1.1 copy.17
  342.7 1.0 fusion.11
  343.7 0.0 copy-start.4
  343.7 0.7 copy-done.4
  344.4 11.7 %cholesky.50 = f32[128,128]{1,0:T(8,128)S(1)} custom-call(f32[128,128]{1,0:T(8,128)S(1)} %cholesky.118), custom_call_target="Cholesky" | custom-call | tf_op jit(solution)/shard_map/jit(cholesky)/cholesky | solution.py:39
  356.1 0.0 copy-start.5
  356.2 0.6 copy-done.5
  356.7 10.4 %custom-call.14 = f32[1,128,128]{1,2,0:T(8,128)} custom-call(f32[1,128,128]{2,1,0:T(8,128)S(1)} %get-tuple-element.29), custom_call_target="InvertDiagBlocksLowerTriangular" | custom-call | tf_op jit(solution)/shard_map/jit(cholesky)/cholesky | solution.py:39
  367.2 0.9 cholesky.113
  368.1 1.1 constant_dynamic-update-slice_fusion.1
  369.1 1.7 convolution_subtract_fusion.1
  370.9 13.4 %cholesky.105 = f32[128,128]{1,0:T(8,128)} custom-call(f32[128,128]{1,0:T(8,128)} %convolution_subtract_fusion.1), custom_call_target="Cholesky" | custom-call | tf_op jit(solution)/shard_map/jit(cholesky)/cholesky | solution.py:39
  384.3 0.9 select_reduce_fusion
  385.1 0.0 copy-start.2
  385.1 0.7 compare_reduce_fusion
  387.2 0.0 copy-done.2
  387.2 1.7 fusion.13
  388.9 0.1 triangular_solve.58
  389.0 5.3 %while.1 = (s32[]{:T(128)}, f32[256,256]{1,0:T(8,128)S(1)}, s32[2,2]{1,0:T(2,128)S(1)}, f32[2,128,128]{2,1,0:T(8,128)}, s32[]{:T(128)}) while((s32[]{:T(128)}, f32[256,256]{1,0:T(8,128)S(1)}, s32[2,2]{1,0:T(2,128)S(1)}, f32[2,128,128]{2,1,0:T(8,128)}, s32[]{:T(128)}) %tuple.30), condition=%wide.while_cond, body=%wide.while_body.sunk | while | flops 2 | bytes 132705 | solution.py:40
  389.0 0.6 fusion.27
  389.6 2.1 bitcast_dynamic-update-slice_fusion.2
  391.7 0.6 fusion.27
  392.3 2.0 bitcast_dynamic-update-slice_fusion.2
  394.3 21.1 %custom-call.15 = f32[2,128,128]{1,2,0:T(8,128)} custom-call(f32[2,128,128]{2,1,0:T(8,128)} %get-tuple-element.9), custom_call_target="InvertDiagBlocksLowerTriangular" | custom-call | tf_op jit(solution)/shard_map/triangular_solve | solution.py:40
  415.4 1.9 fusion.8
  417.4 0.0 copy-start.6
  417.4 1.8 convolution_subtract_fusion
  419.2 0.0 copy-done.6
  419.2 1.1 fusion.14
  420.3 0.1 pad_maximum_fusion.1
  420.4 0.0 copy-start.3
  420.5 1.8 copy.18
  422.3 0.0 copy-done.3
  422.3 0.8 copy.19
  (10 shorter events, 0.1 us)
Async XLA Ops:
  7.2 47.3 %copy-start = (bf16[9,256,256]{2,1,0:T(8,128)(2,1)S(1)}, bf16[9,256,256]{2,1,0:T(8,128)(2,1)}, u32[]{:S(2)}) copy-start(bf16[9,256,256]{2,1,0:T(8,128)(2,1)} %param.6) | copy-start | bytes 3538948
  7.2 10.0 %copy-start.7 = (f32[2048]{0:T(1024)S(1)}, f32[2048]{0:T(1024)}, u32[]{:S(2)}) copy-start(f32[2048]{0:T(1024)} %param.5) | copy-start | bytes 24580
  7.2 10.1 %copy-start.8 = (s32[8,9]{1,0:T(8,128)S(1)}, s32[8,9]{1,0:T(8,128)}, u32[]{:S(2)}) copy-start(s32[8,9]{1,0:T(8,128)} %param.7) | copy-start | bytes 868
  7.2 334.4 %all-reduce.3.cloned.1.call-start = ((), (), s32[]{:S(2)}) async-start(), calls=%async_computation | async-start | bytes 524288 | tf_op jit(solution)/shard_map/psum | solution.py:38
  8.9 24.1 %collective-permute-start = (bf16[2048,256]{1,0:T(8,128)(2,1)S(1)}, bf16[2048,256]{1,0:T(8,128)(2,1)S(1)}, u32[]{:S(2)}, u32[]{:S(2)}) collective-permute-start(bf16[2048,256]{1,0:T(8,128)(2,1)S(1)} %multiply_convert_fusion), channel_id=1, source_target_pairs={{0,1},{1,2},{2,3},{3,4},{4,5},{5,6},{6,7},{7,8},{8,9},{9,10},{10,1... | collective-permute-start | bytes 3145736 | tf_op jit(solution)/shard_map/ppermute | solution.py:12
  15.3 28.6 %collective-permute-start.1 = (bf16[2048,256]{1,0:T(8,128)(2,1)S(1)}, bf16[2048,256]{1,0:T(8,128)(2,1)}, u32[]{:S(2)}, u32[]{:S(2)}) collective-permute-start(bf16[2048,256]{1,0:T(8,128)(2,1)S(1)} %multiply_convert_fusion), channel_id=1, source_target_pairs={{1,0},{2,1},{3,2},{4,3},{5,4},{6,5},{7,6},{8,7},{9,8},{10,9},{11,1... | collective-permute-start | bytes 3145736 | tf_op jit(solution)/shard_map/ppermute | solution.py:15
  59.9 1.3 copy-start.1
  343.7 0.7 copy-start.4
  356.1 0.6 copy-start.5
  385.1 2.1 copy-start.2
  417.4 1.8 copy-start.6
  420.4 1.8 copy-start.3
Sparse Core Ops, SparseCore 0:
  66.2 275.3 all-reduce.2
where the time goes:
time: 431 us; the launch traced here: 430 us
  waiting for transfers between devices  300 us (70%)
  other arithmetic  67.5 us (16%)
  local copies, waits for them, and re-layouts  20.7 us (5%)
  matrix products  17.9 us (4%)
  between operations  15.6 us (4%)
  starting transfers between devices  8.33 us (2%)
    psum x1, waiting for transfers between devices, per_device(): gram_matrix = lax.psum(gram_matrix, ('grp', 'dev'))  274 us
    another operation x6, other arithmetic, per_device(): lower_factor = jnp.linalg.cholesky(gram_matrix)  37.2 us
    another operation x3, other arithmetic, per_device(): lax.linalg.triangular_solve(lower_factor, latent_field, left_side=False,...  21.2 us
    ppermute x1, waiting for transfers between devices, with_halo(): lax.ppermute(lax.slice_in_dim(block, block.shape[dim] - width, None, axis...  15.5 us
    ppermute x1, waiting for transfers between devices, with_halo(): lax.ppermute(lax.slice_in_dim(block, 0, width, axis=dim), axis, backward)  10.8 us
  transfers between devices with their start and end apart: 3, of which 3 were waited for; matrix products, arithmetic and copies ran while one was open for 1% of the time, Pallas kernels for 0%

commit v1 on v0

--- a/solution.py
+++ b/solution.py
@@ -35,7 +35,7 @@
     gram_matrix = (
         jnp.dot(latent_field.T, latent_field, precision=lax.Precision.HIGHEST) / total_rows
     )
-    gram_matrix = lax.psum(gram_matrix, ("grp", "dev"))
+    gram_matrix = lax.psum(lax.psum(gram_matrix, "dev"), "grp")
     lower_factor = jnp.linalg.cholesky(gram_matrix)
     basis = lax.linalg.triangular_solve(
         lower_factor, latent_field, left_side=False, lower=True, transpose_a=True

time: 431 us -> 593 us (1.38)
  the two profiles are of different devices: /device:TPU:23 before, /device:TPU:2 now
where the time goes in v1:
time: 593 us; the launch traced here: 592 us
  waiting for transfers between devices  458 us (77%)
  other arithmetic  67.3 us (11%)
  local copies, waits for them, and re-layouts  20.7 us (3%)
  matrix products  17.7 us (3%)
  between operations  15.6 us (3%)
  starting transfers between devices  12.5 us (2%)
    psum x2, waiting for transfers between devices, per_device(): gram_matrix = lax.psum(lax.psum(gram_matrix, 'dev'), 'grp')  435 us
    another operation x6, other arithmetic, per_device(): lower_factor = jnp.linalg.cholesky(gram_matrix)  37 us
    another operation x3, other arithmetic, per_device(): lax.linalg.triangular_solve(lower_factor, latent_field, left_side=False,...  21.2 us
    ppermute x1, waiting for transfers between devices, with_halo(): lax.ppermute(lax.slice_in_dim(block, 0, width, axis=dim), axis, backward)  13 us
  transfers between devices with their start and end apart: 4, of which 4 were waited for; matrix products, arithmetic and copies ran while one was open for 0% of the time, Pallas kernels for 0%

profile of v1, /device:TPU:2, one launch (start us, length us, event | category | flops | bytes accessed | tf_op | source)
XLA Modules:
  0.0 591.8 jit_solution(1049853280138594572)
XLA Ops:
  7.2 0.0 copy-start
  7.2 0.0 copy-start.7
  7.2 0.0 copy-start.8
  7.2 0.0 all-reduce.4.cloned.1.call-start
  7.2 1.6 multiply_convert_fusion
  8.9 1.9 collective-permute-start
  10.8 10.3 %collective-permute-start.1 = (bf16[2048,256]{1,0:T(8,128)(2,1)S(1)}, bf16[2048,256]{1,0:T(8,128)(2,1)}, u32[]{:S(2)}, u32[]{:S(2)}) collective-permute-start(bf16[2048,256]{1,0:T(8,128)(2,1)S(1)} %multiply_convert_fusion), channel_id=1, source_target_pairs={{1,0},{2,1},{3,2},{4,3},{5,4},{6,5},{7,6},{8,7},{9,8},{10,9},{11,1... | collective-permute-start | bytes 3145736 | tf_op jit(solution)/shard_map/ppermute | solution.py:15
  21.2 0.0 copy-done.7
  21.2 0.0 copy-done.8
  21.2 0.1 copy.13
  21.3 0.1 reshape.62
  21.4 0.1 copy.12
  21.5 10.3 %collective-permute-done = bf16[2048,256]{1,0:T(8,128)(2,1)S(1)} collective-permute-done((bf16[2048,256]{1,0:T(8,128)(2,1)S(1)}, bf16[2048,256]{1,0:T(8,128)(2,1)S(1)}, u32[]{:S(2)}, u32[]{:S(2)}) %collective-permute-start) | collective-permute-done | bytes 1048608 | tf_op jit(solution)/shard_map/ppermute | solution.py:12
  31.9 13.0 %collective-permute-done.1 = bf16[2048,256]{1,0:T(8,128)(2,1)} collective-permute-done((bf16[2048,256]{1,0:T(8,128)(2,1)S(1)}, bf16[2048,256]{1,0:T(8,128)(2,1)}, u32[]{:S(2)}, u32[]{:S(2)}) %collective-permute-start.1) | collective-permute-done | bytes 1048608 | tf_op jit(solution)/shard_map/ppermute | solution.py:15
  44.9 2.8 pad_maximum_fusion
  47.7 7.8 %gather_fusion = bf16[72,256,256]{2,1,0:T(8,128)(2,1)} fusion(bf16[24,256,256]{2,1,0:T(8,128)(2,1)} %bitcast.60, s32[1024]{0:T(1024)S(1)} %pad_clamp_fusion), kind=kCustom, calls=%fused_computation | custom fusion | bytes 18874656 | tf_op jit(solution)/shard_map/gather | solution.py:30
  55.5 0.0 copy-done
  55.5 5.3 fusion
  60.8 0.0 copy-start.1
  60.8 1.3 copy-done.1
  62.1 4.8 fusion.7
  66.9 0.0 all-reduce.4.cloned.1.call-update
  67.0 0.2 all-reduce.6.cloned.1.call-start
  67.2 281.9 %all-reduce.4.cloned.1.call-done = f32[256,256]{0,1:T(8,128)} async-done(((f32[256,256]{0,1:T(8,128)}), f32[256,256]{0,1:T(8,128)}) %all-reduce.4.cloned.1.call-update) | async-done | bytes 262160 | tf_op jit(solution)/shard_map/psum | solution.py:38
  349.1 0.0 all-reduce.6.cloned.1.call-update
  349.2 1.9 bitcast_multiply_fusion
  351.1 152.6 %all-reduce.6.cloned.1.call-done = f32[256,256]{0,1:T(8,128)} async-done(((f32[256,256]{0,1:T(8,128)}), f32[256,256]{0,1:T(8,128)}) %all-reduce.6.cloned.1.call-update) | async-done | bytes 262160 | tf_op jit(solution)/shard_map/psum | solution.py:38
  503.7 1.1 copy.17
  504.8 1.0 fusion.11
  505.8 0.0 copy-start.4
  505.8 0.7 copy-done.4
  506.5 11.7 %cholesky.50 = f32[128,128]{1,0:T(8,128)S(1)} custom-call(f32[128,128]{1,0:T(8,128)S(1)} %cholesky.118), custom_call_target="Cholesky" | custom-call | tf_op jit(solution)/shard_map/jit(cholesky)/cholesky | solution.py:39
  518.2 0.0 copy-start.5
  518.3 0.6 copy-done.5
  518.9 10.4 %custom-call.14 = f32[1,128,128]{1,2,0:T(8,128)} custom-call(f32[1,128,128]{2,1,0:T(8,128)S(1)} %get-tuple-element.29), custom_call_target="InvertDiagBlocksLowerTriangular" | custom-call | tf_op jit(solution)/shard_map/jit(cholesky)/cholesky | solution.py:39
  529.3 0.9 cholesky.113
  530.2 1.1 constant_dynamic-update-slice_fusion.1
  531.2 1.7 convolution_subtract_fusion.1
  533.0 13.2 %cholesky.105 = f32[128,128]{1,0:T(8,128)} custom-call(f32[128,128]{1,0:T(8,128)} %convolution_subtract_fusion.1), custom_call_target="Cholesky" | custom-call | tf_op jit(solution)/shard_map/jit(cholesky)/cholesky | solution.py:39
  546.2 0.9 select_reduce_fusion
  547.0 0.0 copy-start.2
  547.0 0.7 compare_reduce_fusion
  549.1 0.0 copy-done.2
  549.1 1.7 fusion.13
  550.8 0.1 triangular_solve.58
  550.9 5.3 while.1
  550.9 0.6 fusion.27
  551.5 2.1 bitcast_dynamic-update-slice_fusion.2
  553.5 0.6 fusion.27
  554.1 2.1 bitcast_dynamic-update-slice_fusion.2
  556.2 21.1 %custom-call.15 = f32[2,128,128]{1,2,0:T(8,128)} custom-call(f32[2,128,128]{2,1,0:T(8,128)} %get-tuple-element.9), custom_call_target="InvertDiagBlocksLowerTriangular" | custom-call | tf_op jit(solution)/shard_map/triangular_solve | solution.py:40
  577.3 1.9 fusion.8
  579.2 0.0 copy-start.6
  579.2 1.8 convolution_subtract_fusion
  581.1 0.0 copy-done.6
  581.1 1.1 fusion.14
  582.2 0.1 pad_maximum_fusion.1
  582.3 0.0 copy-start.3
  582.3 1.8 copy.18
  584.2 0.0 copy-done.3
  584.2 0.8 copy.19
  (10 shorter events, 0.1 us)
Async XLA Ops:
  7.2 48.3 %copy-start = (bf16[9,256,256]{2,1,0:T(8,128)(2,1)S(1)}, bf16[9,256,256]{2,1,0:T(8,128)(2,1)}, u32[]{:S(2)}) copy-start(bf16[9,256,256]{2,1,0:T(8,128)(2,1)} %param.6) | copy-start | bytes 3538948
  7.2 14.0 %copy-start.7 = (f32[2048]{0:T(1024)S(1)}, f32[2048]{0:T(1024)}, u32[]{:S(2)}) copy-start(f32[2048]{0:T(1024)} %param.5) | copy-start | bytes 24580
  7.2 14.0 %copy-start.8 = (s32[8,9]{1,0:T(8,128)S(1)}, s32[8,9]{1,0:T(8,128)}, u32[]{:S(2)}) copy-start(s32[8,9]{1,0:T(8,128)} %param.7) | copy-start | bytes 868
  7.2 341.9 %all-reduce.4.cloned.1.call-start = ((), (), s32[]{:S(2)}) async-start(), calls=%async_computation | async-start | bytes 524288 | tf_op jit(solution)/shard_map/psum | solution.py:38
  8.9 23.0 %collective-permute-start = (bf16[2048,256]{1,0:T(8,128)(2,1)S(1)}, bf16[2048,256]{1,0:T(8,128)(2,1)S(1)}, u32[]{:S(2)}, u32[]{:S(2)}) collective-permute-start(bf16[2048,256]{1,0:T(8,128)(2,1)S(1)} %multiply_convert_fusion), channel_id=1, source_target_pairs={{0,1},{1,2},{2,3},{3,4},{4,5},{5,6},{6,7},{7,8},{8,9},{9,10},{10,1... | collective-permute-start | bytes 3145736 | tf_op jit(solution)/shard_map/ppermute | solution.py:12
  10.8 34.0 %collective-permute-start.1 = (bf16[2048,256]{1,0:T(8,128)(2,1)S(1)}, bf16[2048,256]{1,0:T(8,128)(2,1)}, u32[]{:S(2)}, u32[]{:S(2)}) collective-permute-start(bf16[2048,256]{1,0:T(8,128)(2,1)S(1)} %multiply_convert_fusion), channel_id=1, source_target_pairs={{1,0},{2,1},{3,2},{4,3},{5,4},{6,5},{7,6},{8,7},{9,8},{10,9},{11,1... | collective-permute-start | bytes 3145736 | tf_op jit(solution)/shard_map/ppermute | solution.py:15
  60.8 1.3 copy-start.1
  67.0 436.8 %all-reduce.6.cloned.1.call-start = ((), (), s32[]{:S(2)}) async-start(), calls=%async_computation.1 | async-start | bytes 524288 | tf_op jit(solution)/shard_map/psum | solution.py:38
  505.8 0.7 copy-start.4
  518.2 0.6 copy-start.5
  547.0 2.1 copy-start.2
  579.2 1.8 copy-start.6
  582.3 1.8 copy-start.3
Sparse Core Ops, SparseCore 0:
  67.1 281.9 all-reduce.3
  352.0 151.6 all-reduce.5
